TPU v7x, 1024 devices: a whole 8x8x8 slice. The times are simulated.
1024 devices in a mesh: blk: 64 (over y, x), section: 16 (over z, core).
Axes of the slice: x: 8, y: 8, z: 8, core: 2. Of those that a mesh axis runs over, the one named last changes fastest.
Arguments:
- stream_sent: bfloat16 [16, 256, 3072], P('section', 'blk'), may hold values from -6 to 6
- grad_sent: bfloat16 [16, 256, 3072], P('section', 'blk'), may hold values from -3 to 3
- preact_now: bfloat16 [16, 256, 16384], P('section', None, 'blk'), may hold values from -16 to 16
- preact_back: bfloat16 [16, 256, 16384], P('section', None, 'blk'), may hold values from -6 to 6
- down_weight: bfloat16 [16, 16384, 3072], P('section', 'blk'), may hold values from -0.109375 to 0.109375
- block_mask: int32 [16, 128, 24], P('section', 'blk'), may hold values from 0 to 1, as said below
Outputs:
- stream_out: bfloat16 [16, 256, 3072], P('section', 'blk')
- preact_grad: bfloat16 [16, 256, 16384], P('section', None, 'blk')
- weight_grad: bfloat16 [16, 16384, 3072], P('section', 'blk')
Inputs may be any that keep to these rules, and one draw needn't show every extreme that they name: `block_mask`: 1 marks a nonzero 128 x 128 block of the down projection, 0 an empty one.
All inputs are finite; a program needn't handle non-finite values.
Results may differ from a plain program's by a relative error of at most 0.005.
Values may be sent and summed in bfloat16 or wider, within the bound.
A program may use at most 32 MiB of HBM per device.

v0:
```python
import jax
import jax.numpy as jnp
from jax import lax
from jax.sharding import PartitionSpec as P

BLOCK = 128


def shifted(block, axis, distance):
    devices = range(lax.axis_size(axis))
    route = [(i - distance, i) for i in devices if i - distance in devices]
    return lax.ppermute(block, axis, route)


def expand(blocks):
    values = blocks.astype(jnp.bfloat16)
    return jnp.repeat(jnp.repeat(values, BLOCK, axis=0), BLOCK, axis=1)


def body(stream_sent, grad_sent, preact_now, preact_back, down_weight, block_mask):
    section_index = lax.axis_index("section")
    final_section = lax.axis_size("section") - 1
    expanded = expand(block_mask[0])
    masked = down_weight[0] * expanded
    arrived = shifted(stream_sent, "section", 1)
    stream = jnp.where(section_index == 0, stream_sent, arrived)[0]
    hidden_now = jax.nn.gelu(preact_now[0].astype(jnp.float32)).astype(jnp.bfloat16)
    summed = lax.psum_scatter(
        jnp.dot(hidden_now, masked, preferred_element_type=jnp.float32),
        "blk",
        scatter_dimension=0,
        tiled=True,
    )
    stream_out = (stream.astype(jnp.float32) + summed).astype(jnp.bfloat16)[None]
    arrived = shifted(grad_sent, "section", -1)
    grad = jnp.where(section_index == final_section, grad_sent, arrived)[0]
    gathered = lax.all_gather(grad, "blk", axis=0, tiled=True)
    grad_hidden = lax.dot_general(
        gathered, masked, (((1,), (1,)), ((), ())), preferred_element_type=jnp.float32
    )
    preact_f = preact_back[0].astype(jnp.float32)
    hidden_f, pullback = jax.vjp(jax.nn.gelu, preact_f)
    preact_grad = pullback(grad_hidden)[0].astype(jnp.bfloat16)
    hidden_back = hidden_f.astype(jnp.bfloat16)
    weight_full = lax.dot_general(
        hidden_back, gathered, (((0,), (0,)), ((), ())), preferred_element_type=jnp.float32
    )
    weight_grad = (weight_full * expanded.astype(jnp.float32)).astype(jnp.bfloat16)
    preact_grad, weight_grad = (preact_grad[None], weight_grad[None])
    return (stream_out, preact_grad, weight_grad)


def solution(mesh):
    placed = (
        P("section", "blk", None),
        P("section", "blk", None),
        P("section", None, "blk"),
        P("section", None, "blk"),
        P("section", "blk", None),
        P("section", "blk", None),
    )
    return jax.shard_map(
        body,
        mesh=mesh,
        in_specs=placed,
        out_specs=(P("section", "blk", None), P("section", None, "blk"), P("section", "blk", None)),
        check_vma=False,
    )
```

profile of v0, /device:TPU:14, one launch (start us, length us, event | category | flops | bytes accessed | tf_op | source)
XLA Modules:
  0.0 303.3 jit_solution(13970228527048000408)
XLA Ops:
  7.2 0.0 all-gather.3.cloned.1.call-start
  7.2 0.8 copy.12
  8.0 1.3 collective-permute-start.1
  9.3 1.8 collective-permute-done.1
  11.1 1.4 broadcast_select_fusion
  12.5 0.0 all-gather.3.cloned.1.call-update
  12.6 0.0 all-reduce.3.cloned.1.call-start
  12.6 0.7 convert_bitcast_fusion
  13.3 1.0 broadcast_in_dim.16
  14.3 0.0 copy-start.1
  14.3 0.7 reshape.23
  15.0 0.2 copy-done.1
  15.2 3.7 %fusion.6 = f32[256,3072]{1,0:T(8,128)} fusion(bf16[1,256,3072]{2,1,0:T(8,128)(2,1)} %param.10, bf16[1,256,3072]{2,1,0:T(8,128)(2,1)S(1)} %reshape.23, bf16[1,256,256]{2,1,0:T(8,128)(2,1)S(1)} %copy-done.1), kind=kOutput, calls=%fused_computation.8 | convolution fusion | flops 404094976 | bytes 6422528 | tf_op jit(solution)/shard_map/dot_general | solution.py:29
  19.0 0.0 copy-start.2
  19.0 0.0 copy-start
  19.0 0.0 copy-start.4
  19.0 0.0 all-reduce.3.cloned.1.call-update
  19.0 0.7 copy-done.2
  19.7 5.8 %collective-permute-start = (bf16[1,4,3072]{2,1,0:T(4,128)(2,1)S(1)}, bf16[1,4,3072]{2,1,0:T(4,128)(2,1)S(1)}, u32[]{:S(2)}, u32[]{:S(2)}) collective-permute-start(bf16[1,4,3072]{2,1,0:T(4,128)(2,1)S(1)} %copy-done.2), channel_id=1, source_target_pairs={{0,1},{1,2},{2,3},{3,4},{4,5},{5,6},{6,7},{7,8},{8,9},{9,10},{10,1... | collective-permute-start | bytes 73736 | tf_op jit(solution)/shard_map/ppermute | solution.py:12
  25.6 1.3 dynamic-slice
  27.5 87.4 %all-gather.3.cloned.1.call-done = bf16[1,256,3072]{2,0,1:T(2,128)(2,1)} async-done(((bf16[1,4,3072]{2,0,1:T(2,128)(2,1)}), bf16[1,256,3072]{2,0,1:T(2,128)(2,1)}) %all-gather.3.cloned.1.call-update) | async-done | bytes 1572880 | tf_op jit(solution)/shard_map/all_gather | solution.py:37
  114.9 0.0 copy-done
  114.9 0.0 copy-done.4
  114.9 0.0 copy-start.3
  114.9 3.5 %fusion.30 = bf16[1,256,256]{2,1,0:T(8,128)(2,1)} fusion(bf16[1,256,3072]{2,1,0:T(8,128)(2,1)S(1)} %copy-done, bf16[32,8,24,128]{3,2,1,0:T(8,128)(2,1)S(1)} %bitcast.53, bf16[1,256,3072]{2,0,1:T(2,128)(2,1)} %all-gather.3.cloned.1.call-done, bf16[1,256,256]{2,1,0:T(8,128)(2,1)S(1)} %copy-done.4), kind=kOutput, calls=%fused_computation.39 | convolution fusion | flops 404815872 | bytes 4980736 | tf_op jit(solution)/shard_map/dot_general | solution.py:38
  118.5 0.0 copy-done.3
  118.5 2.1 fusion.1
  120.5 0.0 collective-permute-done
  120.5 174.4 %all-reduce.3.cloned.1.call-done = f32[256,3072]{1,0:T(8,128)} async-done(((f32[256,3072]{1,0:T(8,128)}), f32[256,3072]{1,0:T(8,128)}) %all-reduce.3.cloned.1.call-update) | async-done | bytes 3145744
  295.0 1.5 fusion.46
  (1 shorter events, 0.0 us)
Async XLA Ops:
  7.2 107.8 %all-gather.3.cloned.1.call-start = ((), (), s32[]{:S(2)}) async-start(), calls=%async_computation | async-start | bytes 3194880 | tf_op jit(solution)/shard_map/all_gather | solution.py:37
  8.0 3.1 %collective-permute-start.1 = (bf16[1,4,3072]{2,0,1:T(2,128)(2,1)S(1)}, bf16[1,4,3072]{2,0,1:T(2,128)(2,1)S(1)}, u32[]{:S(2)}, u32[]{:S(2)}) collective-permute-start(bf16[1,4,3072]{2,0,1:T(2,128)(2,1)S(1)} %copy.12), channel_id=1, source_target_pairs={{1,0},{2,1},{3,2},{4,3},{5,4},{6,5},{7,6},{8,7},{9,8},{10,9},{11,1... | collective-permute-start | bytes 73736 | tf_op jit(solution)/shard_map/ppermute | solution.py:12
  12.6 282.4 %all-reduce.3.cloned.1.call-start = ((), (), s32[]{:S(2)}) async-start(), calls=%async_computation.1 | async-start | bytes 6291456
  14.3 0.9 copy-start.1
  19.0 0.7 copy-start.2
  19.0 96.0 %copy-start = (bf16[1,256,3072]{2,1,0:T(8,128)(2,1)S(1)}, bf16[1,256,3072]{2,1,0:T(8,128)(2,1)}, u32[]{:S(2)}) copy-start(bf16[1,256,3072]{2,1,0:T(8,128)(2,1)} %param.10) | copy-start | bytes 4718596
  19.0 96.0 %copy-start.4 = (bf16[1,256,256]{2,1,0:T(8,128)(2,1)S(1)}, bf16[1,256,256]{2,1,0:T(8,128)(2,1)}, u32[]{:S(2)}) copy-start(bf16[1,256,256]{2,1,0:T(8,128)(2,1)} %param.9) | copy-start | bytes 393220
  19.7 100.8 %collective-permute-start = (bf16[1,4,3072]{2,1,0:T(4,128)(2,1)S(1)}, bf16[1,4,3072]{2,1,0:T(4,128)(2,1)S(1)}, u32[]{:S(2)}, u32[]{:S(2)}) collective-permute-start(bf16[1,4,3072]{2,1,0:T(4,128)(2,1)S(1)} %copy-done.2), channel_id=1, source_target_pairs={{0,1},{1,2},{2,3},{3,4},{4,5},{5,6},{6,7},{7,8},{8,9},{9,10},{10,1... | collective-permute-start | bytes 73736 | tf_op jit(solution)/shard_map/ppermute | solution.py:12
  114.9 3.5 %copy-start.3 = (bf16[1,256,3072]{2,0,1:T(2,128)(2,1)S(1)}, bf16[1,256,3072]{2,0,1:T(2,128)(2,1)}, u32[]{:S(2)}) copy-start(bf16[1,256,3072]{2,0,1:T(2,128)(2,1)} %all-gather.3.cloned.1.call-done) | copy-start | bytes 4718596
Sparse Core Ops, SparseCore 0:
  12.7 102.1 all-gather.2
  118.2 176.7 all-reduce.2
where the time goes:
time: 305 us; the launch traced here: 303 us
  waiting for transfers between devices  264 us (87%)
  between operations  14.8 us (5%)
  matrix products  9.34 us (3%)
  starting transfers between devices  7.21 us (2%)
  local copies, waits for them, and re-layouts  4.65 us (2%)
  other arithmetic  3.64 us (1%)
    unnamed x3, waiting for transfers between devices  174 us
    all_gather x1, waiting for transfers between devices, body(): gathered = lax.all_gather(grad, 'blk', axis=0, tiled=True)  87.4 us
    ppermute x2, starting transfers between devices, shifted(): return lax.ppermute(block, axis, route)  7.13 us
  transfers between devices with their start and end apart: 4, of which 3 were waited for; matrix products, arithmetic and copies ran while one was open for 4% of the time, Pallas kernels for 0%

commit v1 on v0

v1 whole, which is shorter than its diff:
```python
import functools
import math

import jax
import jax.numpy as jnp
from jax import lax
from jax.experimental import pallas as pl
from jax.experimental.pallas import tpu as pltpu
from jax.sharding import PartitionSpec as P

BLOCK = 128
SUBS = 2
MESH = pl.DeviceIdType.MESH
GELU_C = math.sqrt(2.0 / math.pi)
GELU_A = 0.044715
F32 = jnp.float32
BF16 = jnp.bfloat16


def gelu(v):
    return v * (0.5 * (1.0 + jnp.tanh(GELU_C * (v + GELU_A * (v * v * v)))))


def gelu_and_slope(v):
    squared = v * v
    t = jnp.tanh(GELU_C * (v + GELU_A * (squared * v)))
    share = 0.5 * (1.0 + t)
    slope = share + v * (0.5 * (1.0 - t * t) * (GELU_C * (1.0 + 3.0 * GELU_A * squared)))
    return v * share, slope


def dot(a, b):
    return jnp.dot(a, b, preferred_element_type=F32)


def kernel(
    n, sections, stream_ref, grad_ref, now_ref, back_ref, w_ref, mask_ref,
    out_ref, pg_ref, wg_ref,
    mask_s, w_v, now_v, back_v, own_grad, own_stream, part32, part16, hop_in, hop_out, pieces, gathered,
    fan_out, fan_in, slope_v, hidden_t, gh_v, out_v, pg_v, wg_v,
    load_sem, hop_send, hop_recv, ring_send, ring_recv, piece_send, piece_recv, fan_send, fan_recv, relay_sem, store_sem,
):
    hidden, width = w_v.shape
    half = width // 2
    sub = half // SUBS
    tokens = gathered.shape[1]
    mine = own_grad.shape[0]
    rows = n * mine
    reach = n // 2
    blk = lax.axis_index("blk")
    section = lax.axis_index("section")
    place = (lax.rem(blk, n), lax.div(blk, n))

    def wrap(v):
        return lax.rem(v + 2 * n, n)

    def device(axis, at, where):
        index = place[1] * n + at if axis == 0 else at * n + place[0]
        return {"blk": index, "section": where}

    def half_columns(h):
        return pl.ds(h * half, half)

    def sub_columns(c):
        return pl.ds(c * sub, sub)

    def block_rows(b):
        return pl.ds(pl.multiple_of(b * rows, rows), rows)

    barrier = pltpu.get_barrier_semaphore()
    for offset in range(1, n):
        for axis in range(2):
            at = wrap(place[axis] + offset)
            pl.semaphore_signal(barrier, inc=1, device_id=device(axis, at, section), device_id_type=MESH)

    @pl.when(section < sections - 1)
    def _():
        pl.semaphore_signal(barrier, inc=1, device_id=device(0, place[0], section + 1), device_id_type=MESH)
        for offset in range(1, n):
            for axis in range(2):
                at = wrap(place[axis] + offset)
                pl.semaphore_signal(barrier, inc=1, device_id=device(axis, at, section + 1), device_id_type=MESH)

    @pl.when(section > 0)
    def _():
        pl.semaphore_signal(barrier, inc=1, device_id=device(0, place[0], section - 1), device_id_type=MESH)

    loads = [
        pltpu.make_async_copy(now_ref.at[0], now_v, load_sem.at[0]),
        pltpu.make_async_copy(mask_ref.at[0], mask_s, load_sem.at[1]),
        pltpu.make_async_copy(grad_ref.at[0], own_grad, load_sem.at[2]),
        pltpu.make_async_copy(back_ref.at[0], back_v, load_sem.at[3]),
    ]
    w_loads = []
    for chunk in range(2 * SUBS):
        columns = pl.ds(chunk * sub, sub)
        w_loads.append(pltpu.make_async_copy(w_ref.at[0, :, columns], w_v.at[:, columns], load_sem.at[4 + chunk]))
    for copy in loads[:2] + w_loads + loads[2:]:
        copy.start()

    def mask_tile(i, j):
        return jnp.full((BLOCK, BLOCK), mask_s[i, j].astype(F32), F32)

    to_row = lax.broadcasted_iota(jnp.int32, (tokens, tokens), 0)
    from_row = lax.broadcasted_iota(jnp.int32, (tokens, tokens), 1)
    shift_rows, shift_mine = rows.bit_length() - 1, mine.bit_length() - 1
    wanted = (
        ((to_row & (rows - 1)) >> shift_mine) * rows + (to_row >> shift_rows) * mine + (to_row & (mine - 1))
    )
    permute = jnp.where(from_row == wanted, 1.0, 0.0).astype(BF16)

    loads[0].wait()
    hidden_now = gelu(now_v[...].astype(F32)).astype(BF16)
    hidden_half = (dot(permute, hidden_now).astype(BF16), hidden_now)
    loads[1].wait()
    for chunk in range(2 * SUBS):
        w_loads[chunk].wait()
        for j in range(chunk * sub // BLOCK, (chunk + 1) * sub // BLOCK):
            for i in range(hidden // BLOCK):
                tile = (pl.ds(i * BLOCK, BLOCK), pl.ds(j * BLOCK, BLOCK))
                w_v[tile] = w_v[tile] * mask_tile(i, j).astype(BF16)
        h, c = divmod(chunk, SUBS)
        product = dot(hidden_half[h], w_v[:, chunk * sub : (chunk + 1) * sub])
        part32[h, :, c * sub : (c + 1) * sub] = product
        part16[h, :, c * sub : (c + 1) * sub] = product.astype(BF16)
    loads[2].wait()

    first, last = section == 0, section == sections - 1
    expected = 2 * (n - 1) + jnp.where(first, 0, 2 * n - 1) + jnp.where(last, 0, 1)
    pl.semaphore_wait(barrier, expected)

    def piece_copy(h, offset, where, slot):
        return pltpu.make_async_remote_copy(
            src_ref=own_grad.at[:, half_columns(h)],
            dst_ref=pieces.at[h, place[h]],
            send_sem=piece_send.at[slot, h, offset],
            recv_sem=piece_recv.at[h, place[h]],
            device_id=device(h, wrap(place[h] + offset), where),
            device_id_type=MESH,
        )

    order = sorted(range(1, n), key=lambda offset: -min(offset, n - offset))
    before = jnp.maximum(section - 1, 0)
    after = jnp.minimum(section + 1, sections - 1)

    @pl.when(section > 0)
    def _():
        for offset in order + [0]:
            for h in range(2):
                piece_copy(h, offset, before, 0).start()

    own_pieces = [
        pltpu.make_async_copy(own_grad.at[:, half_columns(h)], pieces.at[h, place[h]], relay_sem.at[2 + h])
        for h in range(2)
    ]

    @pl.when(last)
    def _():
        for offset in order:
            for h in range(2):
                piece_copy(h, offset, section, 1).start()
        for copy in own_pieces:
            copy.start()

    steps_of = lambda c, way: reach if (c + way) % 2 == 0 else reach - 1
    chains = [(h, c, way) for c in range(SUBS) for h in range(2) for way in range(2)]

    def hop_copy(h, c, way, step):
        turn = 1 - 2 * way
        target = wrap(place[h] + turn * (steps_of(c, way) - step + 1))
        if step == 1:
            source = part16.at[h, block_rows(target), sub_columns(c)]
        else:
            source = hop_out.at[h, way, step - 2, :, sub_columns(c)]
        return pltpu.make_async_remote_copy(
            src_ref=source,
            dst_ref=hop_in.at[h, way, step - 1, :, sub_columns(c)],
            send_sem=hop_send.at[h, c, way, step - 1],
            recv_sem=hop_recv.at[h, c, way, step - 1],
            device_id=device(h, wrap(place[h] + turn), section),
            device_id_type=MESH,
        )

    for h, c, way in chains:
        if steps_of(c, way) >= 1:
            hop_copy(h, c, way, 1).start()

    relay_copy = pltpu.make_async_remote_copy(
        src_ref=stream_ref.at[0],
        dst_ref=own_stream,
        send_sem=relay_sem.at[0],
        recv_sem=relay_sem.at[1],
        device_id=device(0, place[0], after),
        device_id_type=MESH,
    )
    stream_copy = pltpu.make_async_copy(stream_ref.at[0], own_stream, relay_sem.at[4])

    @pl.when(section < sections - 1)
    def _():
        relay_copy.start()

    @pl.when(first)
    def _():
        stream_copy.start()

    loads[3].wait()
    hidden_back, slope = gelu_and_slope(back_v[...].astype(F32))
    slope_v[...] = slope
    transposed = jnp.transpose(hidden_back).astype(BF16)
    hidden_t[0] = transposed
    hidden_t[1] = dot(transposed, permute).astype(BF16)

    def ring_copy(h, c, way, step):
        turn = 1 - 2 * way
        region = gathered.at[h, block_rows(wrap(place[1 - h] - turn * (step - 1))), sub_columns(c)]
        return pltpu.make_async_remote_copy(
            src_ref=region,
            dst_ref=region,
            send_sem=ring_send.at[h, c, way, step - 1],
            recv_sem=ring_recv.at[h, c, way, step - 1],
            device_id=device(1 - h, wrap(place[1 - h] + turn), section),
            device_id_type=MESH,
        )

    def ring_arrival(h, c, way, step):
        turn = 1 - 2 * way
        region = gathered.at[h, block_rows(wrap(place[1 - h] - turn * step)), sub_columns(c)]
        return pltpu.make_async_remote_copy(
            src_ref=region,
            dst_ref=region,
            send_sem=ring_send.at[h, c, way, step - 1],
            recv_sem=ring_recv.at[h, c, way, step - 1],
            device_id=device(1 - h, wrap(place[1 - h] + turn), section),
            device_id_type=MESH,
        )

    def piece_arrival(h, at):
        return pltpu.make_async_remote_copy(
            src_ref=own_grad.at[:, half_columns(h)],
            dst_ref=pieces.at[h, at],
            send_sem=piece_send.at[0, h, 0],
            recv_sem=piece_recv.at[h, at],
            device_id=device(0, place[0], after),
            device_id_type=MESH,
        )

    @pl.when(last)
    def _():
        for copy in own_pieces:
            copy.wait()

    @pl.when(section < sections - 1)
    def _():
        for h in range(2):
            piece_arrival(h, place[h]).wait_recv()

    for h in range(2):
        for offset in range(1, n):
            piece_arrival(h, wrap(place[h] + offset)).wait_recv()
        block = jnp.concatenate([pieces[h, at].astype(F32) for at in range(n)], axis=0)
        gathered[h, block_rows(place[1 - h]), :] = block.astype(BF16)
        for c in range(SUBS):
            for way in range(2):
                if steps_of(c, way) >= 1:
                    ring_copy(h, c, way, 1).start()

    for step in range(2, reach + 1):
        for h, c, way in chains:
            if steps_of(c, way) >= step:
                turn = 1 - 2 * way
                hop_copy(h, c, way, step - 1).wait_recv()
                target = wrap(place[h] + turn * (steps_of(c, way) - step + 1))
                cols = slice(c * sub, (c + 1) * sub)
                total = hop_in[h, way, step - 2, :, cols].astype(F32) + part32[h, block_rows(target), cols]
                hop_out[h, way, step - 2, :, cols] = total.astype(BF16)
                hop_copy(h, c, way, step).start()
        for h, c, way in chains:
            if steps_of(c, way) >= step:
                ring_arrival(h, c, way, step - 1).wait_recv()
                ring_copy(h, c, way, step).start()

    def fan_copy(h, offset):
        at = wrap(place[1 - h] + offset)
        return pltpu.make_async_remote_copy(
            src_ref=fan_out.at[h, at],
            dst_ref=fan_in.at[h, place[1 - h]],
            send_sem=fan_send.at[h, offset],
            recv_sem=fan_recv.at[h, place[1 - h]],
            device_id=device(1 - h, at, section),
            device_id_type=MESH,
        )

    for h in range(2):
        for c in range(SUBS):
            cols = slice(c * sub, (c + 1) * sub)
            total = part32[h, block_rows(place[h]), cols]
            for way in range(2):
                if steps_of(c, way) >= 1:
                    hop_copy(h, c, way, steps_of(c, way)).wait_recv()
                    total = total + hop_in[h, way, steps_of(c, way) - 1, :, cols].astype(F32)
            for at in range(n):
                fan_out[h, at, :, cols] = total[at * mine : (at + 1) * mine, :]
        for offset in order:
            fan_copy(h, offset).start()

    for h, c, way in chains:
        if steps_of(c, way) >= 1:
            ring_arrival(h, c, way, steps_of(c, way)).wait_recv()

    contract_last = (((1,), (1,)), ((), ()))
    gh_v[1] = lax.dot_general(gathered[1], w_v[:, half:], contract_last, preferred_element_type=F32)
    gh_v[0] = lax.dot_general(gathered[0], w_v[:, :half], contract_last, preferred_element_type=F32)
    pack = 16 // mine
    for group in range(tokens // 16):
        found = []
        for part in range(pack):
            along_y, along_x = divmod(group * pack + part, n)
            found.append(gh_v[1, pl.ds(along_x * rows + along_y * mine, mine), :])
        here = pl.ds(group * 16, 16)
        pg_v[here, :] = ((gh_v[0, here, :] + jnp.concatenate(found, axis=0)) * slope_v[here, :]).astype(BF16)
    stores = [pltpu.make_async_copy(pg_v, pg_ref.at[0], store_sem.at[0])]
    stores[0].start()
    for chunk in range(2 * SUBS):
        h, c = divmod(chunk, SUBS)
        product = dot(hidden_t[h], gathered[h, :, c * sub : (c + 1) * sub])
        for j in range(sub // BLOCK):
            for i in range(hidden // BLOCK):
                column = chunk * sub // BLOCK + j
                tile = product[i * BLOCK : (i + 1) * BLOCK, j * BLOCK : (j + 1) * BLOCK] * mask_tile(i, column)
                wg_v[pl.ds(i * BLOCK, BLOCK), pl.ds(column * BLOCK, BLOCK)] = tile.astype(BF16)
        columns = pl.ds(chunk * sub, sub)
        stores.append(pltpu.make_async_copy(wg_v.at[:, columns], wg_ref.at[0, :, columns], store_sem.at[1 + chunk]))
        stores[-1].start()

    @pl.when(section < sections - 1)
    def _():
        relay_copy.wait_send()

    @pl.when(section > 0)
    def _():
        relay_copy.wait_recv()

    @pl.when(first)
    def _():
        stream_copy.wait()

    for h in range(2):
        for offset in range(1, n):
            at = wrap(place[1 - h] + offset)
            pltpu.make_async_remote_copy(
                src_ref=fan_out.at[h, at],
                dst_ref=fan_in.at[h, at],
                send_sem=fan_send.at[h, offset],
                recv_sem=fan_recv.at[h, at],
                device_id=device(1 - h, at, section),
                device_id_type=MESH,
            ).wait_recv()
        total = own_stream[:, h * half : (h + 1) * half].astype(F32) + fan_out[h, place[1 - h]]
        for offset in range(1, n):
            total = total + fan_in[h, wrap(place[1 - h] + offset)]
        out_v[:, h * half : (h + 1) * half] = total.astype(BF16)
    stores.append(pltpu.make_async_copy(out_v, out_ref.at[0], store_sem.at[1 + 2 * SUBS]))
    stores[-1].start()

    @pl.when(section > 0)
    def _():
        for offset in range(n):
            for h in range(2):
                piece_copy(h, offset, before, 0).wait_send()

    @pl.when(last)
    def _():
        for offset in range(1, n):
            for h in range(2):
                piece_copy(h, offset, section, 1).wait_send()

    for h, c, way in chains:
        for step in range(1, steps_of(c, way) + 1):
            hop_copy(h, c, way, step).wait_send()
            ring_copy(h, c, way, step).wait_send()
    for h in range(2):
        for offset in range(1, n):
            fan_copy(h, offset).wait_send()
    for copy in stores:
        copy.wait()


def body(n, sections, stream_sent, grad_sent, preact_now, preact_back, down_weight, block_mask):
    mine, width = stream_sent.shape[1:]
    tokens, hidden = preact_now.shape[1:]
    half = width // 2
    rows, reach = n * mine, n // 2
    anywhere = pl.BlockSpec(memory_space=pl.ANY)
    dma = pltpu.SemaphoreType.DMA
    return pl.pallas_call(
        functools.partial(kernel, n, sections),
        name="relay_layer",
        out_shape=(
            jax.ShapeDtypeStruct(stream_sent.shape, BF16),
            jax.ShapeDtypeStruct(preact_back.shape, BF16),
            jax.ShapeDtypeStruct(down_weight.shape, BF16),
        ),
        in_specs=[anywhere] * 6,
        out_specs=(anywhere,) * 3,
        scratch_shapes=[
            pltpu.SMEM(block_mask.shape[1:], jnp.int32),
            pltpu.VMEM((hidden, width), BF16),
            pltpu.VMEM((tokens, hidden), BF16),
            pltpu.VMEM((tokens, hidden), BF16),
            pltpu.VMEM((mine, width), BF16),
            pltpu.VMEM((mine, width), BF16),
            pltpu.VMEM((2, tokens, half), F32),
            pltpu.VMEM((2, tokens, half), BF16),
            pltpu.VMEM((2, 2, reach, rows, half), BF16),
            pltpu.VMEM((2, 2, reach - 1, rows, half), BF16),
            pltpu.VMEM((2, n, mine, half), BF16),
            pltpu.VMEM((2, tokens, half), BF16),
            pltpu.VMEM((2, n, mine, half), F32),
            pltpu.VMEM((2, n, mine, half), F32),
            pltpu.VMEM((tokens, hidden), F32),
            pltpu.VMEM((2, hidden, tokens), BF16),
            pltpu.VMEM((2, tokens, hidden), F32),
            pltpu.VMEM((mine, width), BF16),
            pltpu.VMEM((tokens, hidden), BF16),
            pltpu.VMEM((hidden, width), BF16),
            dma((4 + 2 * SUBS,)),
            dma((2, SUBS, 2, reach)),
            dma((2, SUBS, 2, reach)),
            dma((2, SUBS, 2, reach)),
            dma((2, SUBS, 2, reach)),
            dma((2, 2, n)),
            dma((2, n)),
            dma((2, n)),
            dma((2, n)),
            dma((5,)),
            dma((2 + 2 * SUBS,)),
        ],
        compiler_params=pltpu.CompilerParams(collective_id=0, has_side_effects=True),
    )(stream_sent, grad_sent, preact_now, preact_back, down_weight, block_mask)


def solution(mesh):
    n = math.isqrt(mesh.shape["blk"])
    placed = (
        P("section", "blk", None),
        P("section", "blk", None),
        P("section", None, "blk"),
        P("section", None, "blk"),
        P("section", "blk", None),
        P("section", "blk", None),
    )
    return jax.shard_map(
        functools.partial(body, n, mesh.shape["section"]),
        mesh=mesh,
        in_specs=placed,
        out_specs=(P("section", "blk", None), P("section", None, "blk"), P("section", "blk", None)),
        check_vma=False,
    )
```

time: 305 us -> 50.2 us (0.16)
  the two profiles are of different devices: /device:TPU:14 before, /device:TPU:2 now
where the time goes in v1:
time: 50.2 us; the launch traced here: 50 us
  Pallas kernels  43.7 us (87%)
  local copies, waits for them, and re-layouts  5.57 us (11%)
  between operations  0.64 us (1%)
    pallas_call x1, Pallas kernels, body(): pl.pallas_call(functools.partial(kernel, n, sections), name='relay_layer'...  43.7 us
    unnamed x3, local copies, waits for them, and re-layouts  5.57 us

profile of v1, /device:TPU:2, one launch (start us, length us, event | category | flops | bytes accessed | tf_op | source)
XLA Modules:
  0.0 50.0 jit_solution(12443454395916262683)
XLA Ops:
  0.6 43.7 %relay_layer.1 = (bf16[1,4,3072]{2,1,0:T(4,128)(2,1)}, bf16[1,256,256]{2,1,0:T(8,128)(2,1)}, bf16[1,256,3072]{2,1,0:T(8,128)(2,1)}) custom-call(bf16[1,4,3072]{2,1,0:T(4,128)(2,1)} %stream_ref.1, bf16[1,4,3072]{2,1,0:T(4,128)(2,1)} %grad_ref.1, bf16[1,256,256]{2,1,0:T(8,128)(2,1)} %now_ref.1, bf16[1,256,256]{2,1,0:T(8,128)(2,1)} %back_ref.1, ...), custom_call_target="tpu_custom_call" | custom-call | tf_op jit(solution)/shard_map/relay_layer/pallas_call | solution.py:395
  44.4 1.4 %copy.12 = bf16[1,4,3072]{2,1,0:T(4,128)(2,1)} copy(bf16[1,4,3072]{2,1,0:T(4,128)(2,1)} %get-tuple-element.6) | data formatting | bytes 49152
  45.7 1.6 %copy.13 = bf16[1,256,256]{2,1,0:T(8,128)(2,1)} copy(bf16[1,256,256]{2,1,0:T(8,128)(2,1)} %get-tuple-element.7) | data formatting | bytes 262144
  47.3 2.7 %copy.14 = bf16[1,256,3072]{2,1,0:T(8,128)(2,1)} copy(bf16[1,256,3072]{2,1,0:T(8,128)(2,1)} %get-tuple-element.8) | data formatting | bytes 3145728

commit v2 on v1

v2 whole, which is shorter than its diff:
```python
import functools
import math

import jax
import jax.numpy as jnp
from jax import lax
from jax.experimental import pallas as pl
from jax.experimental.pallas import tpu as pltpu
from jax.sharding import PartitionSpec as P

BLOCK = 128
SUBS = 2
MESH = pl.DeviceIdType.MESH
GELU_C = math.sqrt(2.0 / math.pi)
GELU_A = 0.044715
F32 = jnp.float32
BF16 = jnp.bfloat16


def gelu(v):
    return v * (0.5 * (1.0 + jnp.tanh(GELU_C * (v + GELU_A * (v * v * v)))))


def gelu_and_slope(v):
    squared = v * v
    t = jnp.tanh(GELU_C * (v + GELU_A * (squared * v)))
    share = 0.5 * (1.0 + t)
    slope = share + v * (0.5 * (1.0 - t * t) * (GELU_C * (1.0 + 3.0 * GELU_A * squared)))
    return v * share, slope


def dot(a, b):
    return jnp.dot(a, b, preferred_element_type=F32)


def kernel(
    n, sections, stream_ref, grad_ref, now_ref, back_ref, w_ref, mask_ref,
    out_v, pg_v, wg_v,
    mask_s, w_v, now_v, back_v, own_grad, own_stream, part32, part16, hop_in, hop_out, pieces, gathered,
    fan_out, fan_in, total_v, slope_v, hidden_t, gh_v,
    load_sem, hop_recv, ring_send, ring_recv, piece_send, piece_recv, fan_recv, relay_sem,
):
    hidden, width = w_v.shape
    half = width // 2
    sub = half // SUBS
    tokens = gathered.shape[1]
    mine = own_grad.shape[0]
    rows = n * mine
    reach = n // 2
    blk = lax.axis_index("blk")
    section = lax.axis_index("section")
    place = (lax.rem(blk, n), lax.div(blk, n))

    def wrap(v):
        return lax.rem(v + 2 * n, n)

    def device(axis, at, where):
        index = place[1] * n + at if axis == 0 else at * n + place[0]
        return {"blk": index, "section": where}

    def half_columns(h):
        return pl.ds(h * half, half)

    def sub_columns(c):
        return pl.ds(c * sub, sub)

    def block_rows(b):
        return pl.ds(pl.multiple_of(b * rows, rows), rows)

    loads = [
        pltpu.make_async_copy(now_ref.at[0], now_v, load_sem.at[0]),
        pltpu.make_async_copy(mask_ref.at[0], mask_s, load_sem.at[1]),
        pltpu.make_async_copy(grad_ref.at[0], own_grad, load_sem.at[2]),
        pltpu.make_async_copy(back_ref.at[0], back_v, load_sem.at[3]),
    ]
    w_loads = []
    for chunk in range(2 * SUBS):
        columns = pl.ds(chunk * sub, sub)
        w_loads.append(pltpu.make_async_copy(w_ref.at[0, :, columns], w_v.at[:, columns], load_sem.at[4 + chunk]))
    for copy in loads[:2] + w_loads + loads[2:]:
        copy.start()

    barrier = pltpu.get_barrier_semaphore()
    order = sorted(range(1, n), key=lambda offset: -min(offset, n - offset))
    for offset in order:
        for axis in range(2):
            at = wrap(place[axis] + offset)
            pl.semaphore_signal(barrier, inc=1, device_id=device(axis, at, section), device_id_type=MESH)

    @pl.when(section < sections - 1)
    def _():
        pl.semaphore_signal(barrier, inc=1, device_id=device(0, place[0], section + 1), device_id_type=MESH)
        for offset in order:
            for axis in range(2):
                at = wrap(place[axis] + offset)
                pl.semaphore_signal(barrier, inc=1, device_id=device(axis, at, section + 1), device_id_type=MESH)

    @pl.when(section > 0)
    def _():
        pl.semaphore_signal(barrier, inc=1, device_id=device(0, place[0], section - 1), device_id_type=MESH)

    def mask_tile(i, j):
        return jnp.full((BLOCK, BLOCK), mask_s[i, j].astype(F32), F32)

    to_row = lax.broadcasted_iota(jnp.int32, (tokens, tokens), 0)
    from_row = lax.broadcasted_iota(jnp.int32, (tokens, tokens), 1)
    shift_rows, shift_mine = rows.bit_length() - 1, mine.bit_length() - 1
    wanted = (
        ((to_row & (rows - 1)) >> shift_mine) * rows + (to_row >> shift_rows) * mine + (to_row & (mine - 1))
    )
    permute = jnp.where(from_row == wanted, 1.0, 0.0).astype(BF16)

    loads[0].wait()
    hidden_now = gelu(now_v[...].astype(F32)).astype(BF16)
    hidden_half = (dot(permute, hidden_now).astype(BF16), hidden_now)
    loads[1].wait()
    for chunk in range(2 * SUBS):
        w_loads[chunk].wait()
        for j in range(chunk * sub // BLOCK, (chunk + 1) * sub // BLOCK):
            for i in range(hidden // BLOCK):
                tile = (pl.ds(i * BLOCK, BLOCK), pl.ds(j * BLOCK, BLOCK))
                w_v[tile] = w_v[tile] * mask_tile(i, j).astype(BF16)
        h, c = divmod(chunk, SUBS)
        product = dot(hidden_half[h], w_v[:, chunk * sub : (chunk + 1) * sub])
        part32[h, :, c * sub : (c + 1) * sub] = product
        part16[h, :, c * sub : (c + 1) * sub] = product.astype(BF16)
    loads[2].wait()

    first, last = section == 0, section == sections - 1
    expected = 2 * (n - 1) + jnp.where(first, 0, 2 * n - 1) + jnp.where(last, 0, 1)
    pl.semaphore_wait(barrier, expected)

    def piece_copy(h, offset, where, slot):
        return pltpu.make_async_remote_copy(
            src_ref=own_grad.at[:, half_columns(h)],
            dst_ref=pieces.at[h, place[h]],
            send_sem=piece_send.at[slot],
            recv_sem=piece_recv.at[h],
            device_id=device(h, wrap(place[h] + offset), where),
            device_id_type=MESH,
        )

    before = jnp.maximum(section - 1, 0)
    after = jnp.minimum(section + 1, sections - 1)

    @pl.when(section > 0)
    def _():
        for offset in order + [0]:
            for h in range(2):
                piece_copy(h, offset, before, 0).start()

    own_pieces = [
        pltpu.make_async_copy(own_grad.at[:, half_columns(h)], pieces.at[h, place[h]], relay_sem.at[2 + h])
        for h in range(2)
    ]

    @pl.when(last)
    def _():
        for offset in order:
            for h in range(2):
                piece_copy(h, offset, section, 1).start()
        for copy in own_pieces:
            copy.start()

    steps_of = lambda c, way: reach if (c + way) % 2 == 0 else reach - 1
    chains = [(h, c, way) for c in range(SUBS) for h in range(2) for way in range(2)]

    def hop_copy(h, c, way, step):
        turn = 1 - 2 * way
        target = wrap(place[h] + turn * (steps_of(c, way) - step + 1))
        if step == 1:
            source = part16.at[h, block_rows(target), sub_columns(c)]
        else:
            source = hop_out.at[h, way, step - 2, :, sub_columns(c)]
        return pltpu.make_async_remote_copy(
            src_ref=source,
            dst_ref=hop_in.at[h, way, step - 1, :, sub_columns(c)],
            send_sem=ring_send.at[0],
            recv_sem=hop_recv.at[h, c, way, step - 1],
            device_id=device(h, wrap(place[h] + turn), section),
            device_id_type=MESH,
        )

    for h, c, way in chains:
        if steps_of(c, way) >= 1:
            hop_copy(h, c, way, 1).start()

    relay_copy = pltpu.make_async_remote_copy(
        src_ref=stream_ref.at[0],
        dst_ref=own_stream,
        send_sem=relay_sem.at[0],
        recv_sem=relay_sem.at[1],
        device_id=device(0, place[0], after),
        device_id_type=MESH,
    )
    stream_copy = pltpu.make_async_copy(stream_ref.at[0], own_stream, relay_sem.at[4])

    @pl.when(section < sections - 1)
    def _():
        relay_copy.start()

    @pl.when(first)
    def _():
        stream_copy.start()

    loads[3].wait()
    hidden_back, slope = gelu_and_slope(back_v[...].astype(F32))
    slope_v[...] = slope
    transposed = jnp.transpose(hidden_back).astype(BF16)
    hidden_t[0] = transposed
    hidden_t[1] = dot(transposed, permute).astype(BF16)

    def ring_copy(h, c, way, step):
        turn = 1 - 2 * way
        region = gathered.at[h, block_rows(wrap(place[1 - h] - turn * (step - 1))), sub_columns(c)]
        return pltpu.make_async_remote_copy(
            src_ref=region,
            dst_ref=region,
            send_sem=ring_send.at[1],
            recv_sem=ring_recv.at[h, c, way, step - 1],
            device_id=device(1 - h, wrap(place[1 - h] + turn), section),
            device_id_type=MESH,
        )

    def ring_arrival(h, c, way, step):
        turn = 1 - 2 * way
        region = gathered.at[h, block_rows(wrap(place[1 - h] - turn * step)), sub_columns(c)]
        return pltpu.make_async_remote_copy(
            src_ref=region,
            dst_ref=region,
            send_sem=ring_send.at[1],
            recv_sem=ring_recv.at[h, c, way, step - 1],
            device_id=device(1 - h, wrap(place[1 - h] + turn), section),
            device_id_type=MESH,
        )

    def waiter(region, sem):
        return pltpu.make_async_remote_copy(
            src_ref=region,
            dst_ref=region,
            send_sem=sem,
            recv_sem=sem,
            device_id=device(0, place[0], after),
            device_id_type=MESH,
        )

    def hop_onward(h, c, way, step):
        turn = 1 - 2 * way
        hop_copy(h, c, way, step - 1).wait_recv()
        target = wrap(place[h] + turn * (steps_of(c, way) - step + 1))
        cols = slice(c * sub, (c + 1) * sub)
        total = hop_in[h, way, step - 2, :, cols].astype(F32) + part32[h, block_rows(target), cols]
        hop_out[h, way, step - 2, :, cols] = total.astype(BF16)
        hop_copy(h, c, way, step).start()

    def ring_onward(h, c, way, step):
        ring_arrival(h, c, way, step - 1).wait_recv()
        ring_copy(h, c, way, step).start()

    def start_ring():
        @pl.when(last)
        def _():
            for h in range(2):
                own_pieces[h].wait()
                waiter(pieces.at[h, pl.ds(0, n - 1)], piece_recv.at[h]).wait_recv()

        @pl.when(section < sections - 1)
        def _():
            for h in range(2):
                waiter(pieces.at[h], piece_recv.at[h]).wait_recv()

        for h in range(2):
            block = jnp.concatenate([pieces[h, at].astype(F32) for at in range(n)], axis=0)
            gathered[h, block_rows(place[1 - h]), :] = block.astype(BF16)
        for h, c, way in chains:
            if steps_of(c, way) >= 1:
                ring_copy(h, c, way, 1).start()

    for step in range(2, reach + 1):
        for c in range(SUBS):
            for chain in chains:
                if chain[1] == c and steps_of(*chain[1:]) >= step:
                    hop_onward(*chain, step)
            if step > 2:
                for chain in chains:
                    if chain[1] == c and steps_of(*chain[1:]) >= step - 1:
                        ring_onward(*chain, step - 1)
        if step == 2:
            start_ring()

    def fan_copy(h, offset):
        at = wrap(place[1 - h] + offset)
        return pltpu.make_async_remote_copy(
            src_ref=fan_out.at[h, at],
            dst_ref=fan_in.at[h, place[1 - h]],
            send_sem=ring_send.at[2],
            recv_sem=fan_recv.at[h],
            device_id=device(1 - h, at, section),
            device_id_type=MESH,
        )

    for h in range(2):
        for c in range(SUBS):
            cols = slice(c * sub, (c + 1) * sub)
            total = part32[h, block_rows(place[h]), cols]
            for way in range(2):
                if steps_of(c, way) >= 1:
                    hop_copy(h, c, way, steps_of(c, way)).wait_recv()
                    total = total + hop_in[h, way, steps_of(c, way) - 1, :, cols].astype(F32)
            for at in range(n):
                total_v[h, at, :, cols] = total[at * mine : (at + 1) * mine, :]
                fan_out[h, at, :, cols] = total[at * mine : (at + 1) * mine, :].astype(BF16)
        for offset in order:
            fan_copy(h, offset).start()

    for chain in chains:
        if steps_of(*chain[1:]) >= reach:
            ring_onward(*chain, reach)

    contract_last = (((1,), (1,)), ((), ()))
    for c in range(SUBS):
        for h in range(2):
            for way in range(2):
                if steps_of(c, way) >= 1:
                    ring_arrival(h, c, way, steps_of(c, way)).wait_recv()
            arrived = gathered[h, :, c * sub : (c + 1) * sub]
            start = h * half + c * sub
            product = lax.dot_general(
                arrived, w_v[:, start : start + sub], contract_last, preferred_element_type=F32
            )
            gh_v[h] = product if c == 0 else gh_v[h] + product
            product = dot(hidden_t[h], arrived)
            for j in range(sub // BLOCK):
                for i in range(hidden // BLOCK):
                    column = start // BLOCK + j
                    tile = product[i * BLOCK : (i + 1) * BLOCK, j * BLOCK : (j + 1) * BLOCK] * mask_tile(i, column)
                    wg_v[pl.ds(i * BLOCK, BLOCK), pl.ds(column * BLOCK, BLOCK)] = tile.astype(BF16)
    pack = 16 // mine
    for group in range(tokens // 16):
        found = []
        for part in range(pack):
            along_y, along_x = divmod(group * pack + part, n)
            found.append(gh_v[1, pl.ds(along_x * rows + along_y * mine, mine), :])
        here = pl.ds(group * 16, 16)
        pg_v[here, :] = ((gh_v[0, here, :] + jnp.concatenate(found, axis=0)) * slope_v[here, :]).astype(BF16)

    @pl.when(section < sections - 1)
    def _():
        relay_copy.wait_send()

    @pl.when(section > 0)
    def _():
        relay_copy.wait_recv()

    @pl.when(first)
    def _():
        stream_copy.wait()

    for h in range(2):
        waiter(fan_in.at[h, pl.ds(0, n - 1)], fan_recv.at[h]).wait_recv()
        total = own_stream[:, h * half : (h + 1) * half].astype(F32) + total_v[h, place[1 - h]]
        for offset in range(1, n):
            total = total + fan_in[h, wrap(place[1 - h] + offset)].astype(F32)
        out_v[:, h * half : (h + 1) * half] = total.astype(BF16)

    @pl.when(section > 0)
    def _():
        for h in range(2):
            waiter(pieces.at[h], piece_send.at[0]).wait_send()

    @pl.when(last)
    def _():
        for h in range(2):
            waiter(pieces.at[h, pl.ds(0, n - 1)], piece_send.at[1]).wait_send()

    for h in range(2):
        waiter(gathered.at[h, pl.ds(0, (n - 1) * rows)], ring_send.at[0]).wait_send()
        waiter(gathered.at[h, pl.ds(0, (n - 1) * rows)], ring_send.at[1]).wait_send()
        waiter(fan_in.at[h, pl.ds(0, n - 1)], ring_send.at[2]).wait_send()


def store_kernel(*refs):
    copies = [pltpu.make_async_copy(refs[k], refs[3 + k].at[0], refs[6].at[k]) for k in range(3)]
    for copy in copies:
        copy.start()
    for copy in copies:
        copy.wait()


def body(n, sections, stream_sent, grad_sent, preact_now, preact_back, down_weight, block_mask):
    mine, width = stream_sent.shape[1:]
    tokens, hidden = preact_now.shape[1:]
    half = width // 2
    rows, reach = n * mine, n // 2
    anywhere = pl.BlockSpec(memory_space=pl.ANY)
    dma = pltpu.SemaphoreType.DMA
    held = pl.pallas_call(
        functools.partial(kernel, n, sections),
        name="relay_layer",
        out_shape=(
            pltpu.VMEM((mine, width), BF16),
            pltpu.VMEM((tokens, hidden), BF16),
            pltpu.VMEM((hidden, width), BF16),
        ),
        in_specs=[anywhere] * 6,
        out_specs=(pl.BlockSpec(memory_space=pltpu.VMEM),) * 3,
        scratch_shapes=[
            pltpu.SMEM(block_mask.shape[1:], jnp.int32),
            pltpu.VMEM((hidden, width), BF16),
            pltpu.VMEM((tokens, hidden), BF16),
            pltpu.VMEM((tokens, hidden), BF16),
            pltpu.VMEM((mine, width), BF16),
            pltpu.VMEM((mine, width), BF16),
            pltpu.VMEM((2, tokens, half), F32),
            pltpu.VMEM((2, tokens, half), BF16),
            pltpu.VMEM((2, 2, reach, rows, half), BF16),
            pltpu.VMEM((2, 2, reach - 1, rows, half), BF16),
            pltpu.VMEM((2, n, mine, half), BF16),
            pltpu.VMEM((2, tokens, half), BF16),
            pltpu.VMEM((2, n, mine, half), BF16),
            pltpu.VMEM((2, n, mine, half), BF16),
            pltpu.VMEM((2, n, mine, half), F32),
            pltpu.VMEM((tokens, hidden), F32),
            pltpu.VMEM((2, hidden, tokens), BF16),
            pltpu.VMEM((2, tokens, hidden), F32),
            dma((4 + 2 * SUBS,)),
            dma((2, SUBS, 2, reach)),
            dma((3,)),
            dma((2, SUBS, 2, reach)),
            dma((2,)),
            dma((2,)),
            dma((2,)),
            dma((5,)),
        ],
        compiler_params=pltpu.CompilerParams(collective_id=0, has_side_effects=True),
    )(stream_sent, grad_sent, preact_now, preact_back, down_weight, block_mask)
    return pl.pallas_call(
        store_kernel,
        name="store_outputs",
        out_shape=(
            jax.ShapeDtypeStruct(stream_sent.shape, BF16),
            jax.ShapeDtypeStruct(preact_back.shape, BF16),
            jax.ShapeDtypeStruct(down_weight.shape, BF16),
        ),
        in_specs=[pl.BlockSpec(memory_space=pltpu.VMEM)] * 3,
        out_specs=(anywhere,) * 3,
        scratch_shapes=[dma((3,))],
    )(*[pltpu.with_memory_space_constraint(a, pltpu.VMEM) for a in held])


def solution(mesh):
    n = math.isqrt(mesh.shape["blk"])
    placed = (
        P("section", "blk", None),
        P("section", "blk", None),
        P("section", None, "blk"),
        P("section", None, "blk"),
        P("section", "blk", None),
        P("section", "blk", None),
    )
    return jax.shard_map(
        functools.partial(body, n, mesh.shape["section"]),
        mesh=mesh,
        in_specs=placed,
        out_specs=(P("section", "blk", None), P("section", None, "blk"), P("section", "blk", None)),
        check_vma=False,
    )
```

time: 50.2 us -> 44 us (0.88)
  the two profiles are of different devices: /device:TPU:2 before, /device:TPU:6 now
where the time goes in v2:
time: 44 us; the launch traced here: 43.9 us
  Pallas kernels  43.2 us (98%)
  between operations  0.64 us (1%)
    pallas_call x1, Pallas kernels, body(): pl.pallas_call(functools.partial(kernel, n, sections), name='relay_layer'...  42 us
    pallas_call x1, Pallas kernels, body(): pl.pallas_call(store_kernel, name='store_outputs', out_shape=(jax.ShapeDt...  1.22 us

profile of v2, /device:TPU:6, one launch (start us, length us, event | category | flops | bytes accessed | tf_op | source)
XLA Modules:
  0.0 43.9 jit_solution(11495778944405937269)
XLA Ops:
  0.6 42.0 %relay_layer.1 = (bf16[4,3072]{1,0:T(4,128)(2,1)S(1)}, bf16[256,256]{1,0:T(8,128)(2,1)S(1)}, bf16[256,3072]{1,0:T(8,128)(2,1)S(1)}) custom-call(bf16[1,4,3072]{2,1,0:T(4,128)(2,1)} %stream_ref.1, bf16[1,4,3072]{2,1,0:T(4,128)(2,1)} %grad_ref.1, bf16[1,256,256]{2,1,0:T(8,128)(2,1)} %now_ref.1, bf16[1,256,256]{2,1,0:T(8,128)(2,1)} %back_ref.1, ...), custom_call_target="tpu_custom_call" | custom-call | tf_op jit(solution)/shard_map/relay_layer/pallas_call | solution.py:397
  42.7 1.2 %store_outputs.1 = (bf16[1,4,3072]{2,1,0:T(4,128)(2,1)}, bf16[1,256,256]{2,1,0:T(8,128)(2,1)}, bf16[1,256,3072]{2,1,0:T(8,128)(2,1)}) custom-call(bf16[4,3072]{1,0:T(4,128)(2,1)S(1)} %get-tuple-element.6.refs_0_, bf16[256,256]{1,0:T(8,128)(2,1)S(1)} %get-tuple-element.7.refs_1_, bf16[256,3072]{1,0:T(8,128)(2,1)S(1)} %get-tuple-element.8.refs_2_), custom_call_target="tpu_custom_call" | custom-call | tf_op jit(solution)/shard_map/store_outputs/pallas_call | solution.py:437

commit v3 on v2

--- a/solution.py
+++ b/solution.py
@@ -38,7 +38,7 @@
     out_v, pg_v, wg_v,
     mask_s, w_v, now_v, back_v, own_grad, own_stream, part32, part16, hop_in, hop_out, pieces, gathered,
     fan_out, fan_in, total_v, slope_v, hidden_t, gh_v,
-    load_sem, hop_recv, ring_send, ring_recv, piece_send, piece_recv, fan_recv, relay_sem,
+    load_sem, hop_recv, ring_send, ring_recv, piece_send, piece_recv, fan_recv, relay_sem, late_sem,
 ):
     hidden, width = w_v.shape
     half = width // 2
@@ -82,22 +82,51 @@
 
     barrier = pltpu.get_barrier_semaphore()
     order = sorted(range(1, n), key=lambda offset: -min(offset, n - offset))
-    for offset in order:
-        for axis in range(2):
-            at = wrap(place[axis] + offset)
-            pl.semaphore_signal(barrier, inc=1, device_id=device(axis, at, section), device_id_type=MESH)
-
-    @pl.when(section < sections - 1)
-    def _():
-        pl.semaphore_signal(barrier, inc=1, device_id=device(0, place[0], section + 1), device_id_type=MESH)
+    first, last = section == 0, section == sections - 1
+    in_line = jnp.logical_or(place[0] == 0, place[1] == 0)
+    is_late = jnp.logical_and(first, blk == 0)
+    meets_late = jnp.logical_and(in_line, jnp.logical_and(section <= 1, jnp.logical_not(is_late)))
+    feeds_late = jnp.logical_and(in_line, section == 1)
+
+    def to_late(h, way):
+        onto = wrap(place[h] + 1 - 2 * way) == 0
+        return jnp.logical_and(first, jnp.logical_and(place[1 - h] == 0, onto))
+
+    beside_late = functools.reduce(jnp.logical_or, [to_late(h, way) for h in range(2) for way in range(2)])
+
+    def announce_to_senders(sem):
         for offset in order:
             for axis in range(2):
                 at = wrap(place[axis] + offset)
-                pl.semaphore_signal(barrier, inc=1, device_id=device(axis, at, section + 1), device_id_type=MESH)
+                pl.semaphore_signal(sem, inc=1, device_id=device(axis, at, section), device_id_type=MESH)
+
+        @pl.when(section < sections - 1)
+        def _():
+            pl.semaphore_signal(sem, inc=1, device_id=device(0, place[0], section + 1), device_id_type=MESH)
+            for offset in order:
+                for axis in range(2):
+                    at = wrap(place[axis] + offset)
+                    pl.semaphore_signal(sem, inc=1, device_id=device(axis, at, section + 1), device_id_type=MESH)
+
+    expected = 2 * (n - 1) + jnp.where(first, 0, 2 * n - 1) + jnp.where(last, 0, 1) - jnp.where(meets_late, 1, 0)
+    expected = expected + jnp.where(is_late, 2 * (n - 1), 0)
+
+    @pl.when(jnp.logical_not(is_late))
+    def _():
+        announce_to_senders(barrier)
 
     @pl.when(section > 0)
     def _():
         pl.semaphore_signal(barrier, inc=1, device_id=device(0, place[0], section - 1), device_id_type=MESH)
+
+    @pl.when(jnp.logical_and(feeds_late, blk > 0))
+    def _():
+        pl.semaphore_signal(barrier, inc=1, device_id={"blk": 0, "section": section - 1}, device_id_type=MESH)
+
+    @pl.when(is_late)
+    def _():
+        pl.semaphore_wait(barrier, expected)
+        announce_to_senders(late_sem)
 
     def mask_tile(i, j):
         return jnp.full((BLOCK, BLOCK), mask_s[i, j].astype(F32), F32)
@@ -113,30 +142,33 @@
     loads[0].wait()
     hidden_now = gelu(now_v[...].astype(F32)).astype(BF16)
     hidden_half = (dot(permute, hidden_now).astype(BF16), hidden_now)
+    def forward(c):
+        for h in range(2):
+            chunk = h * SUBS + c
+            w_loads[chunk].wait()
+            for j in range(chunk * sub // BLOCK, (chunk + 1) * sub // BLOCK):
+                for i in range(hidden // BLOCK):
+                    tile = (pl.ds(i * BLOCK, BLOCK), pl.ds(j * BLOCK, BLOCK))
+                    w_v[tile] = w_v[tile] * mask_tile(i, j).astype(BF16)
+            product = dot(hidden_half[h], w_v[:, chunk * sub : (chunk + 1) * sub])
+            part32[h, :, c * sub : (c + 1) * sub] = product
+            part16[h, :, c * sub : (c + 1) * sub] = product.astype(BF16)
+
     loads[1].wait()
-    for chunk in range(2 * SUBS):
-        w_loads[chunk].wait()
-        for j in range(chunk * sub // BLOCK, (chunk + 1) * sub // BLOCK):
-            for i in range(hidden // BLOCK):
-                tile = (pl.ds(i * BLOCK, BLOCK), pl.ds(j * BLOCK, BLOCK))
-                w_v[tile] = w_v[tile] * mask_tile(i, j).astype(BF16)
-        h, c = divmod(chunk, SUBS)
-        product = dot(hidden_half[h], w_v[:, chunk * sub : (chunk + 1) * sub])
-        part32[h, :, c * sub : (c + 1) * sub] = product
-        part16[h, :, c * sub : (c + 1) * sub] = product.astype(BF16)
+    forward(0)
     loads[2].wait()
 
-    first, last = section == 0, section == sections - 1
-    expected = 2 * (n - 1) + jnp.where(first, 0, 2 * n - 1) + jnp.where(last, 0, 1)
-    pl.semaphore_wait(barrier, expected)
-
-    def piece_copy(h, offset, where, slot):
+    @pl.when(jnp.logical_not(is_late))
+    def _():
+        pl.semaphore_wait(barrier, expected)
+
+    def piece_copy(h, at, where, slot):
         return pltpu.make_async_remote_copy(
             src_ref=own_grad.at[:, half_columns(h)],
             dst_ref=pieces.at[h, place[h]],
             send_sem=piece_send.at[slot],
             recv_sem=piece_recv.at[h],
-            device_id=device(h, wrap(place[h] + offset), where),
+            device_id=device(h, at, where),
             device_id_type=MESH,
         )
 
@@ -147,7 +179,12 @@
     def _():
         for offset in order + [0]:
             for h in range(2):
-                piece_copy(h, offset, before, 0).start()
+                at = wrap(place[h] + offset)
+                held_back = jnp.logical_and(section == 1, jnp.logical_and(place[1 - h] == 0, at == 0))
+
+                @pl.when(jnp.logical_not(held_back))
+                def _():
+                    piece_copy(h, at, before, 0).start()
 
     own_pieces = [
         pltpu.make_async_copy(own_grad.at[:, half_columns(h)], pieces.at[h, place[h]], relay_sem.at[2 + h])
@@ -158,11 +195,11 @@
     def _():
         for offset in order:
             for h in range(2):
-                piece_copy(h, offset, section, 1).start()
+                piece_copy(h, wrap(place[h] + offset), section, 1).start()
         for copy in own_pieces:
             copy.start()
 
-    steps_of = lambda c, way: reach if (c + way) % 2 == 0 else reach - 1
+    steps_of = lambda c, way: reach if way == 1 else reach - 1
     chains = [(h, c, way) for c in range(SUBS) for h in range(2) for way in range(2)]
 
     def hop_copy(h, c, way, step):
@@ -181,9 +218,16 @@
             device_id_type=MESH,
         )
 
-    for h, c, way in chains:
-        if steps_of(c, way) >= 1:
-            hop_copy(h, c, way, 1).start()
+    for c in range(SUBS):
+        if c > 0:
+            forward(c)
+        for h in range(2):
+            for way in range(2):
+                if steps_of(c, way) >= 1:
+
+                    @pl.when(jnp.logical_not(to_late(h, way)))
+                    def _():
+                        hop_copy(h, c, way, 1).start()
 
     relay_copy = pltpu.make_async_remote_copy(
         src_ref=stream_ref.at[0],
@@ -276,6 +320,16 @@
             if steps_of(c, way) >= 1:
                 ring_copy(h, c, way, 1).start()
 
+    @pl.when(beside_late)
+    def _():
+        pl.semaphore_wait(late_sem, 1)
+        for h, c, way in chains:
+            if steps_of(c, way) >= 1:
+
+                @pl.when(to_late(h, way))
+                def _():
+                    hop_copy(h, c, way, 1).start()
+
     for step in range(2, reach + 1):
         for c in range(SUBS):
             for chain in chains:
@@ -288,6 +342,15 @@
         if step == 2:
             start_ring()
 
+            @pl.when(feeds_late)
+            def _():
+                pl.semaphore_wait(late_sem, 1)
+                for h in range(2):
+
+                    @pl.when(place[1 - h] == 0)
+                    def _():
+                        piece_copy(h, 0, before, 0).start()
+
     def fan_copy(h, offset):
         at = wrap(place[1 - h] + offset)
         return pltpu.make_async_remote_copy(
@@ -298,6 +361,10 @@
             device_id=device(1 - h, at, section),
             device_id_type=MESH,
         )
+
+    @pl.when(jnp.logical_and(meets_late, jnp.logical_not(jnp.logical_or(feeds_late, beside_late))))
+    def _():
+        pl.semaphore_wait(late_sem, 1)
 
     for h in range(2):
         for c in range(SUBS):
@@ -431,6 +498,7 @@
             dma((2,)),
             dma((2,)),
             dma((5,)),
+            pltpu.SemaphoreType.REGULAR,
         ],
         compiler_params=pltpu.CompilerParams(collective_id=0, has_side_effects=True),
     )(stream_sent, grad_sent, preact_now, preact_back, down_weight, block_mask)

time: 44 us -> 41.6 us (0.945)
  the two profiles are of different devices: /device:TPU:6 before, /device:TPU:14 now
where the time goes in v3:
time: 41.6 us; the launch traced here: 41.5 us
  Pallas kernels  40.8 us (98%)
  between operations  0.64 us (2%)
    pallas_call x1, Pallas kernels, body(): pl.pallas_call(functools.partial(kernel, n, sections), name='relay_layer'...  39.6 us
    pallas_call x1, Pallas kernels, body(): pl.pallas_call(store_kernel, name='store_outputs', out_shape=(jax.ShapeDt...  1.22 us

profile of v3, /device:TPU:14, one launch (start us, length us, event | category | flops | bytes accessed | tf_op | source)
XLA Modules:
  0.0 41.5 jit_solution(6003754842609124913)
XLA Ops:
  0.6 39.6 %relay_layer.1 = (bf16[4,3072]{1,0:T(4,128)(2,1)S(1)}, bf16[256,256]{1,0:T(8,128)(2,1)S(1)}, bf16[256,3072]{1,0:T(8,128)(2,1)S(1)}) custom-call(bf16[1,4,3072]{2,1,0:T(4,128)(2,1)} %stream_ref.1, bf16[1,4,3072]{2,1,0:T(4,128)(2,1)} %grad_ref.1, bf16[1,256,256]{2,1,0:T(8,128)(2,1)} %now_ref.1, bf16[1,256,256]{2,1,0:T(8,128)(2,1)} %back_ref.1, ...), custom_call_target="tpu_custom_call" | custom-call | tf_op jit(solution)/shard_map/relay_layer/pallas_call | solution.py:464
  40.2 1.2 %store_outputs.1 = (bf16[1,4,3072]{2,1,0:T(4,128)(2,1)}, bf16[1,256,256]{2,1,0:T(8,128)(2,1)}, bf16[1,256,3072]{2,1,0:T(8,128)(2,1)}) custom-call(bf16[4,3072]{1,0:T(4,128)(2,1)S(1)} %get-tuple-element.6.refs_0_, bf16[256,256]{1,0:T(8,128)(2,1)S(1)} %get-tuple-element.7.refs_1_, bf16[256,3072]{1,0:T(8,128)(2,1)S(1)} %get-tuple-element.8.refs_2_), custom_call_target="tpu_custom_call" | custom-call | tf_op jit(solution)/shard_map/store_outputs/pallas_call | solution.py:505

commit v4 on v3

--- a/solution.py
+++ b/solution.py
@@ -199,7 +199,8 @@
         for copy in own_pieces:
             copy.start()
 
-    steps_of = lambda c, way: reach if way == 1 else reach - 1
+    steps_of = lambda c, way: reach if (c + way) % 2 == 0 else reach - 1
+    ring_steps_of = lambda c, way: reach if way == 1 else reach - 1
     chains = [(h, c, way) for c in range(SUBS) for h in range(2) for way in range(2)]
 
     def hop_copy(h, c, way, step):
@@ -317,7 +318,7 @@
             block = jnp.concatenate([pieces[h, at].astype(F32) for at in range(n)], axis=0)
             gathered[h, block_rows(place[1 - h]), :] = block.astype(BF16)
         for h, c, way in chains:
-            if steps_of(c, way) >= 1:
+            if ring_steps_of(c, way) >= 1:
                 ring_copy(h, c, way, 1).start()
 
     @pl.when(beside_late)
@@ -337,7 +338,7 @@
                     hop_onward(*chain, step)
             if step > 2:
                 for chain in chains:
-                    if chain[1] == c and steps_of(*chain[1:]) >= step - 1:
+                    if chain[1] == c and ring_steps_of(*chain[1:]) >= step - 1:
                         ring_onward(*chain, step - 1)
         if step == 2:
             start_ring()
@@ -381,15 +382,15 @@
             fan_copy(h, offset).start()
 
     for chain in chains:
-        if steps_of(*chain[1:]) >= reach:
+        if ring_steps_of(*chain[1:]) >= reach:
             ring_onward(*chain, reach)
 
     contract_last = (((1,), (1,)), ((), ()))
     for c in range(SUBS):
         for h in range(2):
             for way in range(2):
-                if steps_of(c, way) >= 1:
-                    ring_arrival(h, c, way, steps_of(c, way)).wait_recv()
+                if ring_steps_of(c, way) >= 1:
+                    ring_arrival(h, c, way, ring_steps_of(c, way)).wait_recv()
             arrived = gathered[h, :, c * sub : (c + 1) * sub]
             start = h * half + c * sub
             product = lax.dot_general(

time: 41.6 us -> 41 us (0.986)
  Pallas kernels: 40.8 us -> 40.2 us
    pallas_call x1, Pallas kernels: 39.6 us -> 38.9 us  [body(): pl.pallas_call(functools.partial(kernel, n, sections), name='relay_layer'...]
where the time goes in v4:
time: 41 us; the launch traced here: 40.8 us
  Pallas kernels  40.2 us (98%)
  between operations  0.64 us (2%)
    pallas_call x1, Pallas kernels, body(): pl.pallas_call(functools.partial(kernel, n, sections), name='relay_layer'...  38.9 us
    pallas_call x1, Pallas kernels, body(): pl.pallas_call(store_kernel, name='store_outputs', out_shape=(jax.ShapeDt...  1.22 us

profile of v4, /device:TPU:14, one launch (start us, length us, event | category | flops | bytes accessed | tf_op | source)
XLA Modules:
  0.0 40.8 jit_solution(6932186544057037164)
XLA Ops:
  0.6 38.9 %relay_layer.1 = (bf16[4,3072]{1,0:T(4,128)(2,1)S(1)}, bf16[256,256]{1,0:T(8,128)(2,1)S(1)}, bf16[256,3072]{1,0:T(8,128)(2,1)S(1)}) custom-call(bf16[1,4,3072]{2,1,0:T(4,128)(2,1)} %stream_ref.1, bf16[1,4,3072]{2,1,0:T(4,128)(2,1)} %grad_ref.1, bf16[1,256,256]{2,1,0:T(8,128)(2,1)} %now_ref.1, bf16[1,256,256]{2,1,0:T(8,128)(2,1)} %back_ref.1, ...), custom_call_target="tpu_custom_call" | custom-call | tf_op jit(solution)/shard_map/relay_layer/pallas_call | solution.py:465
  39.6 1.2 %store_outputs.1 = (bf16[1,4,3072]{2,1,0:T(4,128)(2,1)}, bf16[1,256,256]{2,1,0:T(8,128)(2,1)}, bf16[1,256,3072]{2,1,0:T(8,128)(2,1)}) custom-call(bf16[4,3072]{1,0:T(4,128)(2,1)S(1)} %get-tuple-element.6.refs_0_, bf16[256,256]{1,0:T(8,128)(2,1)S(1)} %get-tuple-element.7.refs_1_, bf16[256,3072]{1,0:T(8,128)(2,1)S(1)} %get-tuple-element.8.refs_2_), custom_call_target="tpu_custom_call" | custom-call | tf_op jit(solution)/shard_map/store_outputs/pallas_call | solution.py:506
